TPU v7x, 32 devices: a whole 2x2x4 slice. The times are simulated.
32 devices in a mesh: dp: 8 (over y, x, core), tensor: 4 (over z).
Axes of the slice: x: 2, y: 2, z: 4, core: 2. Of those that a mesh axis runs over, the one named last changes fastest.
Arguments:
- tokens: bfloat16 [8192, 1024], P('dp'), may hold values from -6 to 6
- cotangent: bfloat16 [8192, 1024], P('dp'), may hold values from -6 to 6
- seq_lengths: int32 [8, 8], P('dp'), may hold values from 0 to 1024, as said below
- norm_gain: float32 [1024], replicated, may hold values from 0.5 to 1.5
- proj_gate: bfloat16 [1024, 2048], P(None, 'tensor'), may hold values from -0.1875 to 0.1875
- proj_value: bfloat16 [1024, 2048], P(None, 'tensor'), may hold values from -0.1875 to 0.1875
- proj_pair: bfloat16 [1024, 256], replicated, may hold values from -0.1875 to 0.1875
- proj_step: bfloat16 [1024, 32], P(None, 'tensor'), may hold values from -0.1875 to 0.1875
- conv_value: float32 [4, 2048], P(None, 'tensor'), may hold values from -3 to 3
- conv_value_bias: float32 [2048], P('tensor'), may hold values from -0.5 to 0.5
- conv_pair: float32 [4, 256], replicated, may hold values from -3 to 3
- conv_pair_bias: float32 [256], replicated, may hold values from -0.5 to 0.5
- step_bias: float32 [32], P('tensor'), may hold values from -4 to -1
- log_rate: float32 [32], P('tensor'), may hold values from 0 to 2.8
- skip_gain: float32 [32], P('tensor'), may hold values from 0.5 to 1.5
- gate_gain: float32 [2048], P('tensor'), may hold values from 0.5 to 1.5
- proj_out: bfloat16 [2048, 1024], P('tensor'), may hold values from -0.125 to 0.125
Outputs:
- block_out: bfloat16 [8192, 1024], P(('dp', 'tensor'))
- grad_tokens: bfloat16 [8192, 1024], P('dp')
- grad_norm_gain: float32 [1024], replicated
- grad_proj_gate: float32 [1024, 2048], P(None, 'tensor')
- grad_proj_value: float32 [1024, 2048], P(None, 'tensor')
- grad_proj_pair: float32 [1024, 256], replicated
- grad_proj_step: float32 [1024, 32], P(None, 'tensor')
- grad_conv_value: float32 [4, 2048], P(None, 'tensor')
- grad_conv_value_bias: float32 [2048], P('tensor')
- grad_conv_pair: float32 [4, 256], replicated
- grad_conv_pair_bias: float32 [256], replicated
- grad_step_bias: float32 [32], P('tensor')
- grad_log_rate: float32 [32], P('tensor')
- grad_skip_gain: float32 [32], P('tensor')
- grad_gate_gain: float32 [2048], P('tensor')
- grad_proj_out: float32 [2048, 1024], P('tensor')
Inputs may be any that keep to these rules, and one draw needn't show every extreme that they name: `seq_lengths`: row p lists the lengths of the sequences packed in order from the first of the 1024 rows of pack p; a zero is an unused slot; each row sums to at most 1024, and rows past that sum are padding.
All inputs are finite; a program needn't handle non-finite values.
Results may differ from a plain program's by a relative error of at most 0.0098.
Values sent between devices are 32-bit elements; how exact they have to be, the bound alone decides.
No kernel may reach another device: no remote copies, remote signals or barrier semaphores. Data moves between devices by JAX's collectives and lax.ppermute only.
A program may use at most 128 MiB of HBM per device.

v0:
```python
from functools import partial
import jax
import jax.numpy as jnp
from jax import lax
from jax.sharding import PartitionSpec as P

D = 1024
GROUP = 256
DI = 2048
epsilon = 1e-05
HIGHEST = lax.Precision.HIGHEST


def segment_ids(lengths_row, row_count):
    bounds = jnp.cumsum(lengths_row)
    position = jnp.arange(row_count, dtype=jnp.int32)
    segment = jnp.sum((position[:, None] >= bounds[None, :]).astype(jnp.int32), axis=1)
    live_mask = (position < bounds[-1]).astype(jnp.float32)
    return (segment, live_mask)


def conv_silu(pre_act, weight, conv_bias, segment):
    row_count = pre_act.shape[0]
    tap_count = weight.shape[0]
    summed = conv_bias[None, :] + weight[tap_count - 1][None, :] * pre_act
    for offset in range(1, tap_count):
        shifted = jnp.pad(pre_act, ((offset, 0), (0, 0)))[:row_count]
        shifted_seg = jnp.pad(segment, (offset, 0), constant_values=-1)[:row_count]
        same_seq = (shifted_seg == segment).astype(jnp.float32)
        summed = summed + weight[tap_count - 1 - offset][None, :] * shifted * same_seq[:, None]
    return jax.nn.silu(summed)


def ssd_gate(gate_pre, value_post, pair_post, step_pre, step_bias, log_rate, skip_gain, segment):
    row_count = value_post.shape[0]
    head_count = step_pre.shape[1]
    head_dim = value_post.shape[1] // head_count
    state_dim = pair_post.shape[1] // 2
    block_count = row_count // GROUP
    step_size = jax.nn.softplus(step_pre + step_bias[None, :])
    rate_per = -jnp.exp(log_rate)
    log_decay = step_size * rate_per[None, :]
    values = value_post.reshape(row_count, head_count, head_dim)
    scaled = (values * step_size[:, :, None]).reshape(block_count, GROUP, head_count, head_dim)
    cumulative = jnp.cumsum(log_decay.reshape(block_count, GROUP, head_count), axis=1)
    seg_blocks = segment.reshape(block_count, GROUP)
    b_blocks = pair_post[:, :state_dim].reshape(block_count, GROUP, state_dim)
    c_blocks = pair_post[:, state_dim:].reshape(block_count, GROUP, state_dim)
    lower_tri = jnp.arange(GROUP)[:, None] >= jnp.arange(GROUP)[None, :]
    same_seq = (seg_blocks[:, :, None] == seg_blocks[:, None, :]) & lower_tri[None]
    log_gap = cumulative[:, :, None, :] - cumulative[:, None, :, :]
    decay_mat = jnp.where(
        same_seq[..., None], jnp.exp(jnp.where(same_seq[..., None], log_gap, 0.0)), 0.0
    )
    scores = jnp.einsum("cin,cjn->cij", c_blocks, b_blocks, precision=HIGHEST)
    weights = scores[..., None] * decay_mat
    intra_out = jnp.einsum("cijh,cjhp->cihp", weights, scaled, precision=HIGHEST)
    before = jnp.concatenate([jnp.full((1,), -1, jnp.int32), seg_blocks[:-1, -1]])
    end_same = (seg_blocks == seg_blocks[:, -1:]).astype(jnp.float32)
    to_end = jnp.exp(cumulative[:, -1:, :] - cumulative) * end_same[:, :, None]
    local_states = jnp.einsum("cjh,cjn,cjhp->chnp", to_end, b_blocks, scaled, precision=HIGHEST)
    carry_in = jnp.exp(cumulative) * (seg_blocks == before[:, None]).astype(jnp.float32)[:, :, None]
    passes = (
        jnp.exp(cumulative[:, -1, :]) * (seg_blocks[:, -1] == before).astype(jnp.float32)[:, None]
    )

    def advance(state_now, inputs):
        c_block, carry_row, local_state, pass_row = inputs
        inter_out = (
            jnp.einsum("in,hnp->ihp", c_block, state_now, precision=HIGHEST) * carry_row[:, :, None]
        )
        return (local_state + pass_row[:, None, None] * state_now, inter_out)

    start_state = jnp.zeros((head_count, state_dim, head_dim), jnp.float32)
    final_state, inter_all = lax.scan(
        advance, start_state, (c_blocks, carry_in, local_states, passes)
    )
    mixed_out = (intra_out + inter_all).reshape(row_count, head_count * head_dim)
    mixed_out = mixed_out + jnp.repeat(skip_gain, head_dim)[None, :] * value_post
    return mixed_out * jax.nn.silu(gate_pre)


def mixer_rest(
    gate_pre,
    value_pre,
    pair_post,
    step_pre,
    conv_value,
    conv_value_bias,
    step_bias,
    log_rate,
    skip_gain,
    segment,
):
    value_post = conv_silu(value_pre, conv_value, conv_value_bias, segment)
    return ssd_gate(
        gate_pre, value_post, pair_post, step_pre, step_bias, log_rate, skip_gain, segment
    )


def per_device(
    tokens,
    cotangent,
    seq_lengths,
    norm_gain,
    proj_gate,
    proj_value,
    proj_pair,
    proj_step,
    conv_value,
    conv_value_bias,
    conv_pair,
    conv_pair_bias,
    step_bias,
    log_rate,
    skip_gain,
    gate_gain,
    proj_out,
):
    row_count = tokens.shape[0]
    segment, live_mask = segment_ids(seq_lengths[0], row_count)
    widened = tokens.astype(jnp.float32)
    scale_in = lax.rsqrt(jnp.mean(widened * widened, axis=1, keepdims=True) + epsilon)
    normed = (widened * scale_in * norm_gain[None, :]).astype(jnp.bfloat16)
    gate_pre = jnp.dot(normed, proj_gate, preferred_element_type=jnp.float32)
    value_pre = jnp.dot(normed, proj_value, preferred_element_type=jnp.float32)
    pair_pre = jnp.dot(normed, proj_pair, preferred_element_type=jnp.float32)
    step_pre = jnp.dot(normed, proj_step, preferred_element_type=jnp.float32)
    pair_post = conv_silu(pair_pre, conv_pair, conv_pair_bias, segment)
    rest_fn = partial(mixer_rest, segment=segment)
    gated_value, rest_back = jax.vjp(
        rest_fn,
        gate_pre,
        value_pre,
        pair_post,
        step_pre,
        conv_value,
        conv_value_bias,
        step_bias,
        log_rate,
        skip_gain,
    )
    square_sum = lax.psum(jnp.sum(gated_value * gated_value, axis=1), "tensor")
    scale_gate = lax.rsqrt(square_sum[:, None] / DI + epsilon)
    gate_out = (gated_value * scale_gate * gate_gain[None, :]).astype(jnp.bfloat16)
    share_rows = row_count // lax.axis_size("tensor")
    first_row = lax.axis_index("tensor") * share_rows
    mixed_rows = lax.psum_scatter(
        jnp.dot(gate_out, proj_out, preferred_element_type=jnp.float32),
        "tensor",
        scatter_dimension=0,
        tiled=True,
    )
    own_rows = lax.dynamic_slice_in_dim(widened, first_row, share_rows, 0)
    own_live = lax.dynamic_slice_in_dim(live_mask, first_row, share_rows, 0)
    block_out = (own_rows + mixed_rows * own_live[:, None]).astype(jnp.bfloat16)
    cot_live = jnp.where(live_mask[:, None] > 0, cotangent, jnp.zeros_like(cotangent))
    grad_proj_out = jnp.dot(gate_out.T, cot_live, preferred_element_type=jnp.float32)
    grad_gate_out = jnp.dot(cot_live, proj_out.T, preferred_element_type=jnp.float32)
    grad_gate_gain = jnp.sum(grad_gate_out * gated_value * scale_gate, axis=0)
    weighted = grad_gate_out * gate_gain[None, :]
    stat_dot = lax.psum(jnp.sum(weighted * gated_value, axis=1), "tensor")[:, None]
    grad_gated = weighted * scale_gate - gated_value * (scale_gate**3 / DI) * stat_dot
    grads_rest = rest_back(grad_gated)
    low_gate = grads_rest[0].astype(jnp.bfloat16)
    low_value = grads_rest[1].astype(jnp.bfloat16)
    low_step = grads_rest[3].astype(jnp.bfloat16)
    grad_proj_gate = jnp.dot(normed.T, low_gate, preferred_element_type=jnp.float32)
    grad_proj_value = jnp.dot(normed.T, low_value, preferred_element_type=jnp.float32)
    grad_proj_step = jnp.dot(normed.T, low_step, preferred_element_type=jnp.float32)
    grad_local = jnp.dot(low_gate, proj_gate.T, preferred_element_type=jnp.float32)
    grad_local = grad_local + jnp.dot(low_value, proj_value.T, preferred_element_type=jnp.float32)
    grad_local = grad_local + jnp.dot(low_step, proj_step.T, preferred_element_type=jnp.float32)
    pair_grad = lax.psum(grads_rest[2], "tensor")
    pair_fn = partial(conv_silu, segment=segment)
    whole_post, pair_back = jax.vjp(pair_fn, pair_pre, conv_pair, conv_pair_bias)
    grad_pair_pre, grad_conv_pair, grad_conv_pair_bias = pair_back(pair_grad)
    low_pair = grad_pair_pre.astype(jnp.bfloat16)
    grad_proj_pair = jnp.dot(normed.T, low_pair, preferred_element_type=jnp.float32)
    grad_normed = lax.psum(grad_local, "tensor")
    grad_normed = grad_normed + jnp.dot(low_pair, proj_pair.T, preferred_element_type=jnp.float32)
    grad_norm_gain = jnp.sum(grad_normed * widened * scale_in, axis=0)
    scaled_grad = grad_normed * norm_gain[None, :]
    row_dot = jnp.sum(scaled_grad * widened, axis=1, keepdims=True)
    grad_wide = scaled_grad * scale_in - widened * (scale_in**3 / D) * row_dot
    grad_tokens = (cotangent.astype(jnp.float32) + grad_wide).astype(jnp.bfloat16)
    totals = lax.psum(
        (
            grad_norm_gain,
            grad_proj_gate,
            grad_proj_value,
            grad_proj_step,
            grads_rest[4],
            grads_rest[5],
            grads_rest[6],
            grads_rest[7],
            grads_rest[8],
            grad_gate_gain,
            grad_proj_out,
            grad_proj_pair,
            grad_conv_pair,
            grad_conv_pair_bias,
        ),
        "dp",
    )
    pair_totals = (totals[11], totals[12], totals[13])
    return (
        block_out,
        grad_tokens,
        totals[0],
        totals[1],
        totals[2],
        pair_totals[0],
        totals[3],
        totals[4],
        totals[5],
        pair_totals[1],
        pair_totals[2],
        totals[6],
        totals[7],
        totals[8],
        totals[9],
        totals[10],
    )


def solution(mesh):
    return jax.shard_map(
        per_device,
        mesh=mesh,
        in_specs=(
            P("dp", None),
            P("dp", None),
            P("dp", None),
            P(),
            P(None, "tensor"),
            P(None, "tensor"),
            P(),
            P(None, "tensor"),
            P(None, "tensor"),
            P("tensor"),
            P(),
            P(),
            P("tensor"),
            P("tensor"),
            P("tensor"),
            P("tensor"),
            P("tensor", None),
        ),
        out_specs=(
            P(("dp", "tensor"), None),
            P("dp", None),
            P(),
            P(None, "tensor"),
            P(None, "tensor"),
            P(),
            P(None, "tensor"),
            P(None, "tensor"),
            P("tensor"),
            P(),
            P(),
            P("tensor"),
            P("tensor"),
            P("tensor"),
            P("tensor"),
            P("tensor", None),
        ),
        check_vma=False,
    )
```

profile of v0, /device:TPU:0, one launch (start us, length us, event | category | flops | bytes accessed | tf_op | source)
XLA Modules:
  0.0 684.8 jit_solution(3664673852586571083)
XLA Ops:
  17.0 2.3 reduce-window.19
  21.1 2.9 fusion.141
  24.0 2.8 fusion.61
  28.2 2.4 reshape.353
  30.5 2.8 copy.116
  33.4 3.2 fusion.142
  40.4 3.0 fusion.79
  44.6 27.7 %while.44 = (s32[]{:T(128)}, f32[8,128,64]{1,2,0:T(8,128)}, f32[4,256,8,64]{1,3,2,0:T(8,128)}, f32[4,8,128,64]{2,3,1,0:T(8,128)}, f32[4,256,8,1]{1,2,3,0:T(8,128...) while((s32[]{:T(128)}, f32[8,128,64]{1,2,0:T(8,128)}, ...), condition=%wide.region_6.7_spmd.clone, body=%wide.region_5.6_spmd.clone.sunk | while | flops 201654272 | bytes 4632367 | solution.py:75
  72.3 2.3 fusion.143
  75.8 10.8 %bitcast_add_fusion.2 = f32[4,256,8,64]{1,3,2,0:T(8,128)} fusion(f32[4,256,8,64]{1,3,2,0:T(8,128)S(1)} %copy-done.90, f32[4,256,8]{1,2,0:T(8,128)S(1)} %get-tuple-element.561, f32[4,256,256]{2,1,0:T(8,128)S(1)} %fusion.143, pred[4,256,256]{2,1,0:T(8,128)(4,1)S(1)} %compare_and_fusion, f32[4,256,8,64]{1,3,2,0:T(8,128)S(1)} %copy.116, ...), kind=kOutput, calls=%fused_computation.96 | convolution fusion | flops 1620049920 | bytes 7667712 | tf_op jit(solution)/shard_map/jvp(cijh,cjhp->cihp)/dot_general | solution.py:57
  86.6 3.8 copy.144
  90.5 5.3 reshape.354
  95.9 6.3 multiply_reduce_fusion.10
  102.2 13.5 %psum.126 = f32[1024]{0:T(1024)S(1)} all-reduce(f32[1024]{0:T(1024)S(1)} %get-tuple-element.558), channel_id=1, replica_groups=mesh['dp'=8,'tensor'=4] {'tensor'}, use_global_device_ids=true, to_apply=%region_8.9 | all-reduce | flops 1024 | bytes 8192 | tf_op jit(solution)/shard_map/psum | solution.py:143
  116.3 6.0 multiply_reduce_fusion.2
  122.4 8.3 %psum.127 = f32[1024]{0:T(1024)S(1)} all-reduce(f32[1024]{0:T(1024)S(1)} %get-tuple-element.477), channel_id=1, replica_groups=mesh['dp'=8,'tensor'=4] {'tensor'}, use_global_device_ids=true, to_apply=%region_11.12 | all-reduce | flops 1024 | bytes 8192 | tf_op jit(solution)/shard_map/psum | solution.py:162
  130.7 6.2 multiply_reduce_fusion.3
  136.9 2.9 copy.121
  139.8 3.3 reshape.324
  145.6 40.1 %while.45 = (s32[]{:T(128)}, f32[8,128,64]{1,2,0:T(8,128)S(1)}, f32[4,256,128]{2,1,0:T(8,128)}, f32[4,256,8]{1,2,0:T(8,128)S(1)}, f32[4,8,128,64]{2,3,1,0:T(8,12...) while((s32[]{:T(128)}, f32[8,128,64]{1,2,0:T(8,128)S(1)}, ...), condition=%wide.region_15.16_spmd.clone, body=%wide.region_12.15_spmd.clone.sunk | while | flops 403634176 | bytes 5301641 | solution.py:75
  145.6 2.1 constant_dynamic-slice_fusion.4
  186.3 6.5 fusion.82
  192.8 3.3 multiply_reduce_fusion.1
  196.1 3.0 copy.127
  199.0 14.8 %fusion.30 = (f32[4,256,8]{1,2,0:T(8,128)}, f32[4,256,8]{1,2,0:T(8,128)}, f32[4,256,256]{2,1,0:T(8,128)S(1)}) fusion(f32[4,256,8]{1,2,0:T(8,128)S(1)} %get-tuple-element.561, f32[4,256,256]{2,1,0:T(8,128)} %copy-done.36, pred[4,256,256]{2,1,0:T(8,128)(4,1)S(1)} %copy-done.40, f32[4,256,8,64]{1,3,2,0:T(8,128)S(1)} %copy-done.4, ...), kind=kOutput, calls=%fused_computation.55 | convolution fusion | flops 1633927168 | bytes 6684672 | tf_op jit(solution)/shard_map/transpose(jvp(cijh,cjhp->cihp))/dot_general | solution.py:57
  213.9 3.0 convolution_add_fusion.2
  216.9 2.7 convolution_add_fusion.1
  225.9 10.6 %reduce-window.21 = f32[4,8,2,128]{3,1,2,0:T(8,128)S(1)} reduce-window(f32[4,8,2,128]{3,1,2,0:T(8,128)} %add_bitcast_fusion, f32[]{:T(128)} %constant.146.clone.1), window={size=1x1x1x128 pad=0_0x0_0x0_0x0_127}, to_apply=%region_20.21 | reduce-window | flops 1040384 | bytes 65540 | tf_op jit(solution)/shard_map/reduce-window.3
  238.6 9.9 %bitcast_add_fusion.1 = f32[4,256,8,64]{1,3,2,0:T(8,128)} fusion(f32[4,256,8,64]{1,3,2,0:T(8,128)} %get-tuple-element.603, f32[4,256,8]{1,2,0:T(8,128)S(1)} %get-tuple-element.561, f32[4,256,256]{2,1,0:T(8,128)} %copy-done.36, pred[4,256,256]{2,1,0:T(8,128)(4,1)S(1)} %copy-done.40, f32[4,8,64,256]{3,0,2,1:T(4,128)S(1)} %bitcast.248, ...), kind=kOutput, calls=%fused_computation.95 | convolution fusion | flops 1620049920 | bytes 7667712 | tf_op jit(solution)/shard_map/transpose(jvp(cijh,cjhp->cihp))/dot_general | solution.py:57
  248.5 4.0 copy.145
  254.1 4.8 reshape.355
  260.5 3.1 copy.126
  263.6 7.2 %multiply_reduce_fusion.7 = (f32[512]{0:T(512)S(1)}, f32[512]{0:T(512)S(1)}, f32[512]{0:T(512)S(1)}, f32[512]{0:T(512)S(1)}, f32[512]{0:T(512)S(1)}, /*index=5*/f32[1024,512]{1,0:T(8,128)S(1)}) fusion(f32[1024,512]{1,0:T(8,128)} %copy-done.21, f32[1024]{0:T(1024)S(1)} %get-tuple-element.598, f32[1024]{0:T(1024)S(1)} %get-tuple-element.597, ...), kind=kLoop, calls=%fused_computation.103 | loop fusion | flops 12580352 | bytes 12607488 | tf_op jit(solution)/shard_map/transpose(jvp())/reduce_sum | solution.py:30
  278.9 2.7 add_add_fusion
  283.3 4.9 fusion.130
  289.7 3.9 fusion.147
  293.7 2.6 fusion.146
  296.3 2.8 fusion.102
  299.1 171.3 %all-reduce.35.cloned.1.call-done = (f32[1024,1024]{1,0:T(8,128)}, f32[1024,256]{1,0:T(8,128)}) async-done(((f32[1024,1024]{1,0:T(8,128)}, f32[1024,256]{1,0:T(8,128)}), (f32[1024,1024]{1,0:T(8,128)}, f32[1024,256]{1,0:T(8,128)})) %all-reduce.35.cloned.1.call-update) | async-done | bytes 5242896 | tf_op jit(solution)/shard_map/psum | solution.py:180
  470.4 3.9 multiply_reduce_fusion.14
  479.7 2.4 convert_element_type.89
  485.2 5.6 fusion.40
  490.8 26.2 %all-reduce.27 = (f32[1024]{0:T(1024)}, f32[1024,8]{0,1:T(8,128)}, f32[4,512]{1,0:T(4,128)}, f32[512]{0:T(512)}, f32[4,256]{1,0:T(4,128)}, /*index=5*/f32[256]{0...) all-reduce(f32[1024]{0:T(1024)S(1)} %get-tuple-element.474, ...), channel_id=1, replica_groups=mesh['dp'=8,'tensor'=4] {'dp'}, use_global_device_ids=true, to_apply=%region_27.28 | all-reduce | flops 13592 | bytes 108736 | tf_op jit(solution)/shard_map/psum | solution.py:187
  517.1 4.6 fusion.37
  521.7 26.8 %reduce-scatter.2.cloned.1.call-done = f32[256,1024]{1,0:T(8,128)} async-done(((f32[1024,1024]{1,0:T(8,128)}), f32[256,1024]{1,0:T(8,128)}) %reduce-scatter.2.cloned.1.call-update) | async-done | bytes 1048592 | tf_op jit(solution)/shard_map/reduce_scatter | solution.py:148
  548.5 2.5 add_convert_fusion
  551.0 118.4 %all-reduce.33.cloned.1.call-done = (f32[1024,512]{1,0:T(8,128)}, f32[1024,512]{1,0:T(8,128)}, f32[1024,256]{1,0:T(8,128)}, f32[512,1024]{1,0:T(8,128)}) async-done(((f32[1024,512]{1,0:T(8,128)}, f32[1024,512]{1,0:T(8,128)}, f32[1024,256]{1,0:T(8,128)}, f32[512,1024]{1,0:T(8,128)}), (f32[1024,512]{1,0:T(8,128)}, f32[1024,512]{1,0:T(8,128)}, f32[1024,256]{1,0:T(8,128)}, ...) | async-done | bytes 7340048 | tf_op jit(solution)/shard_map/psum | solution.py:187
  669.4 3.2 copy.229
  (355 shorter events, 124.7 us)
Async XLA Ops:
  7.2 88.7 %copy-start = (bf16[1024,512]{1,0:T(8,128)(2,1)S(1)}, bf16[1024,512]{1,0:T(8,128)(2,1)}, u32[]{:S(2)}) copy-start(bf16[1024,512]{1,0:T(8,128)(2,1)} %param.25) | copy-start | bytes 3145732
  7.2 6.7 copy-start.1
  7.2 6.1 copy-start.93
  7.2 6.7 copy-start.53
  7.2 463.2 %all-reduce.35.cloned.1.call-start = ((), (), s32[]{:S(2)}) async-start(), calls=%async_computation.3 | async-start | bytes 10485760 | tf_op jit(solution)/shard_map/psum | solution.py:180
  15.8 5.3 copy-start.91
  20.3 3.7 copy-start.55
  33.4 41.6 %copy-start.3 = (f32[4,256,8,64]{1,3,2,0:T(8,128)}, f32[4,256,8,64]{1,3,2,0:T(8,128)S(1)}, u32[]{:S(2)}) copy-start(f32[4,256,8,64]{1,3,2,0:T(8,128)S(1)} %copy.116) | copy-start | bytes 6291460
  33.4 3.2 copy-start.81
  33.4 3.2 copy-start.87
  39.5 5.1 copy-start.12
  44.6 3.3 copy-start.84
  50.8 4.3 copy-start.84
  58.0 4.3 copy-start.84
  65.2 4.3 copy-start.84
  72.3 3.5 copy-start.90
  90.5 5.3 copy-start.88
  90.5 5.4 copy-start.7
  95.9 34.8 %copy-start.66 = (f32[512]{0:T(512)}, f32[512]{0:T(512)S(1)}, u32[]{:S(2)}) copy-start(f32[512]{0:T(512)S(1)} %mul.754) | copy-start | bytes 6148
  95.9 20.4 %copy-start.64 = (f32[512]{0:T(512)S(1)}, f32[512]{0:T(512)}, u32[]{:S(2)}) copy-start(f32[512]{0:T(512)} %param.36) | copy-start | bytes 6148
  116.3 6.1 copy-start.95
  116.3 14.4 %copy-start.9 = (f32[1024,512]{1,0:T(8,128)S(1)}, f32[1024,512]{1,0:T(8,128)}, u32[]{:S(2)}) copy-start(f32[1024,512]{1,0:T(8,128)} %get-tuple-element.563) | copy-start | bytes 6291460
  139.8 5.8 copy-start.17
  185.7 7.1 %copy-start.4 = (f32[4,256,8,64]{1,3,2,0:T(8,128)S(1)}, f32[4,256,8,64]{1,3,2,0:T(8,128)}, u32[]{:S(2)}) copy-start(f32[4,256,8,64]{1,3,2,0:T(8,128)} %copy-done.3) | copy-start | bytes 6291460
  185.7 7.1 %copy-start.13 = (f32[1024,128]{1,0:T(8,128)S(1)}, f32[1024,128]{1,0:T(8,128)}, u32[]{:S(2)}) copy-start(f32[1024,128]{1,0:T(8,128)} %copy-done.12) | copy-start | bytes 1572868
  185.7 7.1 %copy-start.19 = (f32[4,8,128,64]{2,3,1,0:T(8,128)S(1)}, f32[4,8,128,64]{2,3,1,0:T(8,128)}, u32[]{:S(2)}) copy-start(f32[4,8,128,64]{2,3,1,0:T(8,128)} %get-tuple-element.321) | copy-start | bytes 3145732
  199.0 14.9 %copy-start.14 = (f32[1024,128]{1,0:T(8,128)S(1)}, f32[1024,128]{1,0:T(8,128)}, u32[]{:S(2)}) copy-start(f32[1024,128]{1,0:T(8,128)} %copy-done.12) | copy-start | bytes 1572868
  213.9 5.7 copy-start.46
  213.9 5.7 copy-start.52
  216.9 21.7 %copy-start.18 = (f32[4,256,8,64]{1,0,3,2:T(4,128)S(1)}, f32[4,256,8,64]{1,0,3,2:T(4,128)}, u32[]{:S(2)}) copy-start(f32[4,256,8,64]{1,0,3,2:T(4,128)} %get-tuple-element.875) | copy-start | bytes 6291460
  248.5 4.0 copy-start.20
  260.5 3.1 copy-start.10
  260.5 3.1 copy-start.67
  263.6 7.3 %copy-start.59 = (f32[1,512]{1,0:T(1,128)S(1)}, f32[1,512]{1,0:T(1,128)}, u32[]{:S(2)}) copy-start(f32[1,512]{1,0:T(1,128)} %copy-done.58) | copy-start | bytes 6148
  263.6 7.3 %copy-start.61 = (f32[1,512]{1,0:T(1,128)S(1)}, f32[1,512]{1,0:T(1,128)}, u32[]{:S(2)}) copy-start(f32[1,512]{1,0:T(1,128)} %copy-done.60) | copy-start | bytes 6148
  263.6 7.3 %copy-start.63 = (f32[1,512]{1,0:T(1,128)S(1)}, f32[1,512]{1,0:T(1,128)}, u32[]{:S(2)}) copy-start(f32[1,512]{1,0:T(1,128)} %copy-done.62) | copy-start | bytes 6148
  281.7 266.8 %reduce-scatter.2.cloned.1.call-start = ((), (), s32[]{:S(2)}) async-start(), calls=%async_computation.1 | async-start | bytes 5242880 | tf_op jit(solution)/shard_map/reduce_scatter | solution.py:148
  288.2 381.2 %all-reduce.33.cloned.1.call-start = ((), (), s32[]{:S(2)}) async-start(), calls=%async_computation.2 | async-start | bytes 14680064 | tf_op jit(solution)/shard_map/psum | solution.py:187
  289.7 3.9 copy-start.34
  470.4 3.9 copy-start.72
  470.4 3.9 copy-start.74
  470.4 4.0 copy-start.76
  479.7 3.5 copy-start.94
  482.1 3.1 copy-start.48
  482.1 3.1 copy-start.54
  485.2 5.6 copy-start.83
  485.2 31.8 %copy-start.68 = (f32[1024]{0:T(1024)S(1)}, f32[1024]{0:T(1024)}, u32[]{:S(2)}) copy-start(f32[1024]{0:T(1024)} %get-tuple-element.584) | copy-start | bytes 12292
  669.4 3.2 copy-start.30
  (55 other events, 108.8 us)
Sparse Core Ops, SparseCore 0:
  281.8 188.5 all-reduce.34
  472.7 75.7 reduce-scatter.1
  553.2 116.0 all-reduce.32
where the time goes:
time: 696 us; the launch traced here: 685 us
  waiting for transfers between devices  317 us (46%)
  matrix products  124 us (18%)
  local copies, waits for them, and re-layouts  93.4 us (13%)
  other arithmetic  87.7 us (13%)
  blocking collectives  48 us (7%)
  between operations  15.1 us (2%)
    psum x1, waiting for transfers between devices, per_device(): grad_normed = lax.psum(grad_local, 'tensor')  171 us
    psum x1, waiting for transfers between devices, per_device(): lax.psum((grad_norm_gain, grad_proj_gate, grad_proj_value, grad_proj_step...  118 us
    dot_general x3, matrix products, ssd_gate(): jnp.einsum('cijh,cjhp->cihp', weights, scaled, precision=HIGHEST)  35.6 us
    reduce_scatter x1, waiting for transfers between devices, per_device(): lax.psum_scatter(jnp.dot(gate_out, proj_out, preferred_element_type=jnp.f...  26.8 us
    psum x1, blocking collectives, per_device(): lax.psum((grad_norm_gain, grad_proj_gate, grad_proj_value, grad_proj_step...  26.2 us
    unnamed x196, local copies, waits for them, and re-layouts  20.6 us
    another operation x9, other arithmetic  16.7 us
  transfers between devices with their start and end apart: 3, of which 3 were waited for; matrix products, arithmetic and copies ran while one was open for 6% of the time, Pallas kernels for 0%

commit v1 on v0

--- a/solution.py
+++ b/solution.py
@@ -177,7 +177,7 @@
     grad_pair_pre, grad_conv_pair, grad_conv_pair_bias = pair_back(pair_grad)
     low_pair = grad_pair_pre.astype(jnp.bfloat16)
     grad_proj_pair = jnp.dot(normed.T, low_pair, preferred_element_type=jnp.float32)
-    grad_normed = lax.psum(grad_local, "tensor")
+    grad_normed = jnp.sum(lax.all_gather(grad_local, "tensor"), axis=0)
     grad_normed = grad_normed + jnp.dot(low_pair, proj_pair.T, preferred_element_type=jnp.float32)
     grad_norm_gain = jnp.sum(grad_normed * widened * scale_in, axis=0)
     scaled_grad = grad_normed * norm_gain[None, :]

time: 696 us -> 775 us (1.11)
  waiting for transfers between devices: 317 us -> 403 us
  local copies, waits for them, and re-layouts: 93.4 us -> 82.3 us
    all_gather x0 -> x1, waiting for transfers between devices: none -> 286 us  [per_device(): grad_normed = jnp.sum(lax.all_gather(grad_local, 'tensor'), axis=0)]
    psum x1, waiting for transfers between devices: 171 us -> 0.01 us  [per_device(): pair_grad = lax.psum(grads_rest[2], 'tensor')]
    psum x1, waiting for transfers between devices: 118 us -> 71.6 us  [per_device(): lax.psum((grad_norm_gain, grad_proj_gate, grad_proj_value, grad_proj_step...]
    reduce_scatter x1, waiting for transfers between devices: 26.8 us -> 44.9 us  [per_device(): lax.psum_scatter(jnp.dot(gate_out, proj_out, preferred_element_type=jnp.f...]
    reduce_sum x0 -> x1, other arithmetic: none -> 10.3 us  [per_device(): grad_normed = jnp.sum(lax.all_gather(grad_local, 'tensor'), axis=0)]
    unnamed x196 -> x204, local copies, waits for them, and re-layouts: 20.6 us -> 19.7 us
  transfers between devices with their start and end apart: 3 -> 4, of which waited for: 3 -> 3; matrix products, arithmetic and copies ran while one was open for 6% -> 13% of each run, Pallas kernels for 0% -> 0%
where the time goes in v1:
time: 775 us; the launch traced here: 763 us
  waiting for transfers between devices  403 us (52%)
  matrix products  120 us (15%)
  other arithmetic  93.1 us (12%)
  local copies, waits for them, and re-layouts  82.3 us (11%)
  blocking collectives  49.1 us (6%)
  between operations  15.4 us (2%)
    all_gather x1, waiting for transfers between devices, per_device(): grad_normed = jnp.sum(lax.all_gather(grad_local, 'tensor'), axis=0)  286 us
    psum x1, waiting for transfers between devices, per_device(): lax.psum((grad_norm_gain, grad_proj_gate, grad_proj_value, grad_proj_step...  71.6 us
    reduce_scatter x1, waiting for transfers between devices, per_device(): lax.psum_scatter(jnp.dot(gate_out, proj_out, preferred_element_type=jnp.f...  44.9 us
    dot_general x3, matrix products, ssd_gate(): jnp.einsum('cijh,cjhp->cihp', weights, scaled, precision=HIGHEST)  33.7 us
    psum x1, blocking collectives, per_device(): lax.psum((grad_norm_gain, grad_proj_gate, grad_proj_value, grad_proj_step...  27.3 us
    unnamed x204, local copies, waits for them, and re-layouts  19.7 us
  transfers between devices with their start and end apart: 4, of which 3 were waited for; matrix products, arithmetic and copies ran while one was open for 13% of the time, Pallas kernels for 0%

profile of v1, /device:TPU:0, one launch (start us, length us, event | category | flops | bytes accessed | tf_op | source)
XLA Modules:
  0.0 763.2 jit_solution(1655553466612101974)
XLA Ops:
  17.1 2.3 reduce-window.19
  21.1 2.9 fusion.141
  24.1 2.8 fusion.61
  28.2 2.4 reshape.354
  30.6 2.8 copy.116
  33.4 3.2 fusion.142
  40.5 3.1 fusion.79
  44.7 27.7 %while.44 = (s32[]{:T(128)}, f32[8,128,64]{1,2,0:T(8,128)}, f32[4,256,8,64]{1,3,2,0:T(8,128)}, f32[4,8,128,64]{2,3,1,0:T(8,128)}, f32[4,256,8,1]{1,2,3,0:T(8,128...) while((s32[]{:T(128)}, f32[8,128,64]{1,2,0:T(8,128)}, ...), condition=%wide.region_6.7_spmd.clone, body=%wide.region_5.6_spmd.clone.sunk | while | flops 201654272 | bytes 4632367 | solution.py:75
  72.4 2.3 fusion.143
  75.8 10.8 %bitcast_add_fusion.2 = f32[4,256,8,64]{1,3,2,0:T(8,128)} fusion(f32[4,256,8,64]{1,3,2,0:T(8,128)S(1)} %copy-done.94, f32[4,256,8]{1,2,0:T(8,128)S(1)} %get-tuple-element.559, f32[4,256,256]{2,1,0:T(8,128)S(1)} %fusion.143, pred[4,256,256]{2,1,0:T(8,128)(4,1)S(1)} %compare_and_fusion, f32[4,256,8,64]{1,3,2,0:T(8,128)S(1)} %copy.116, ...), kind=kOutput, calls=%fused_computation.96 | convolution fusion | flops 1620049920 | bytes 7667712 | tf_op jit(solution)/shard_map/jvp(cijh,cjhp->cihp)/dot_general | solution.py:57
  86.7 3.8 copy.144
  90.5 5.0 reshape.355
  95.6 6.8 multiply_reduce_fusion.10
  102.4 13.5 %psum.119 = f32[1024]{0:T(1024)S(1)} all-reduce(f32[1024]{0:T(1024)S(1)} %get-tuple-element.556), channel_id=1, replica_groups=mesh['dp'=8,'tensor'=4] {'tensor'}, use_global_device_ids=true, to_apply=%region_8.9 | all-reduce | flops 1024 | bytes 8192 | tf_op jit(solution)/shard_map/psum | solution.py:143
  116.6 5.9 multiply_reduce_fusion.2
  122.5 8.3 %psum.120 = f32[1024]{0:T(1024)S(1)} all-reduce(f32[1024]{0:T(1024)S(1)} %get-tuple-element.477), channel_id=1, replica_groups=mesh['dp'=8,'tensor'=4] {'tensor'}, use_global_device_ids=true, to_apply=%region_11.12 | all-reduce | flops 1024 | bytes 8192 | tf_op jit(solution)/shard_map/psum | solution.py:162
  130.8 6.7 multiply_reduce_fusion.3
  137.5 2.9 copy.121
  140.4 3.2 reshape.324
  143.6 15.1 %fusion.30 = (f32[4,256,8]{1,2,0:T(8,128)}, f32[4,256,8]{1,2,0:T(8,128)}, f32[4,256,256]{2,1,0:T(8,128)}) fusion(f32[4,256,8]{1,2,0:T(8,128)S(1)} %get-tuple-element.559, f32[4,256,256]{2,1,0:T(8,128)} %copy-done.29, pred[4,256,256]{2,1,0:T(8,128)(4,1)} %copy-done.32, f32[4,256,8,64]{1,3,2,0:T(8,128)S(1)} %copy.116, f32[4,256,8]{1,2,0:T(8,128)S(1)} %bitcast.258, ...), kind=kOutput, calls=%fused_computation.55 | convolution fusion | flops 1633927168 | bytes 6684672 | tf_op jit(solution)/shard_map/transpose(jvp(cijh,cjhp->cihp))/dot_general | solution.py:57
  159.4 40.1 %while.45 = (s32[]{:T(128)}, f32[8,128,64]{1,2,0:T(8,128)S(1)}, f32[4,256,128]{2,1,0:T(8,128)S(1)}, f32[4,256,8]{1,2,0:T(8,128)}, f32[4,8,128,64]{2,3,1,0:T(8,12...) while((s32[]{:T(128)}, f32[8,128,64]{1,2,0:T(8,128)S(1)}, ...), condition=%wide.region_15.16_spmd.clone, body=%wide.region_12.15_spmd.clone.sunk | while | flops 403634176 | bytes 5301641 | solution.py:75
  169.4 2.1 constant_dynamic-slice_fusion.4
  199.6 5.5 fusion.82
  210.1 4.5 fusion.130
  214.7 3.2 copy.127
  217.9 3.5 multiply_reduce_fusion.1
  221.5 7.8 %bitcast_add_fusion.1 = f32[4,256,8,64]{1,3,2,0:T(8,128)S(1)} fusion(f32[4,256,8,64]{1,3,2,0:T(8,128)S(1)} %get-tuple-element.601, f32[4,256,8]{1,2,0:T(8,128)S(1)} %get-tuple-element.559, f32[4,256,256]{2,1,0:T(8,128)S(1)} %copy-done.30, pred[4,256,256]{2,1,0:T(8,128)(4,1)S(1)} %copy-done.33, f32[4,8,64,256]{3,0,2,1:T(4,128)S(1)} %bitcast.250, ...), kind=kOutput, calls=%fused_computation.95 | convolution fusion | flops 1620049920 | bytes 7667712 | tf_op jit(solution)/shard_map/transpose(jvp(cijh,cjhp->cihp))/dot_general | solution.py:57
  229.3 2.8 copy.145
  232.0 4.8 reshape.356
  238.4 3.0 copy.126
  242.0 9.9 %reduce-window.21 = f32[4,8,2,128]{3,1,2,0:T(8,128)S(1)} reduce-window(f32[4,8,2,128]{3,1,2,0:T(8,128)S(1)} %add_bitcast_fusion, f32[]{:T(128)} %constant.146.clone.1), window={size=1x1x1x128 pad=0_0x0_0x0_0x0_127}, to_apply=%region_20.21 | reduce-window | flops 1040384 | bytes 65540 | tf_op jit(solution)/shard_map/reduce-window.3
  252.5 2.3 multiply_reduce_fusion.8
  256.3 4.0 multiply_reduce_fusion.7
  265.6 2.8 add_add_fusion
  270.3 3.9 fusion.147
  274.2 2.6 fusion.146
  276.8 2.8 fusion.102
  279.6 4.2 multiply_reduce_fusion.14
  289.0 2.4 convert_element_type.89
  294.4 44.9 %reduce-scatter.2.cloned.1.call-done = f32[256,1024]{1,0:T(8,128)} async-done(((f32[1024,1024]{1,0:T(8,128)}), f32[256,1024]{1,0:T(8,128)}) %reduce-scatter.2.cloned.1.call-update) | async-done | bytes 1048592 | tf_op jit(solution)/shard_map/reduce_scatter | solution.py:148
  339.3 2.5 add_convert_fusion
  341.8 286.4 %all-gather.3.cloned.1.call-done = f32[4096,1024]{1,0:T(8,128)} async-done(((f32[1024,1024]{1,0:T(8,128)}), f32[4096,1024]{1,0:T(8,128)}) %all-gather.3.cloned.1.call-update) | async-done | bytes 16777232 | tf_op jit(solution)/shard_map/all_gather | solution.py:180
  628.2 10.3 %reduce_sum.292 = f32[1024,1024]{1,0:T(8,128)} reduce(f32[4,1024,1024]{2,1,0:T(8,128)} %bitcast.243, f32[]{:T(128)} %constant.146.clone.1), dimensions={0}, to_apply=%region_22.23 | reduce | flops 3145728 | bytes 20971524 | tf_op jit(solution)/shard_map/reduce_sum | solution.py:180
  638.5 5.8 fusion.40
  644.3 27.3 %all-reduce.27 = (f32[1024]{0:T(1024)}, f32[1024,8]{0,1:T(8,128)}, f32[4,512]{1,0:T(4,128)}, f32[512]{0:T(512)}, f32[4,256]{1,0:T(4,128)}, /*index=5*/f32[256]{0...) all-reduce(f32[1024]{0:T(1024)S(1)} %get-tuple-element.474, ...), channel_id=1, replica_groups=mesh['dp'=8,'tensor'=4] {'dp'}, use_global_device_ids=true, to_apply=%region_27.28 | all-reduce | flops 13592 | bytes 108736 | tf_op jit(solution)/shard_map/psum | solution.py:187
  671.6 4.5 fusion.37
  676.2 71.6 %all-reduce.34.cloned.1.call-done = (f32[1024,512]{1,0:T(8,128)}, f32[1024,512]{1,0:T(8,128)}, f32[1024,256]{1,0:T(8,128)}, f32[512,1024]{1,0:T(8,128)}) async-done(((f32[1024,512]{1,0:T(8,128)}, f32[1024,512]{1,0:T(8,128)}, f32[1024,256]{1,0:T(8,128)}, f32[512,1024]{1,0:T(8,128)}), (f32[1024,512]{1,0:T(8,128)}, f32[1024,512]{1,0:T(8,128)}, f32[1024,256]{1,0:T(8,128)}, ...) | async-done | bytes 7340048 | tf_op jit(solution)/shard_map/psum | solution.py:187
  747.8 3.2 copy.229
  (367 shorter events, 114.9 us)
Async XLA Ops:
  7.2 88.4 %copy-start = (bf16[1024,512]{1,0:T(8,128)(2,1)S(1)}, bf16[1024,512]{1,0:T(8,128)(2,1)}, u32[]{:S(2)}) copy-start(bf16[1024,512]{1,0:T(8,128)(2,1)} %param.25) | copy-start | bytes 3145732
  7.2 6.7 copy-start.1
  7.2 6.1 copy-start.97
  7.2 6.7 copy-start.51
  7.2 272.4 %all-reduce.32.cloned.1.call-start = ((), (), s32[]{:S(2)}) async-start(), calls=%async_computation.2 | async-start | bytes 2097152 | tf_op jit(solution)/shard_map/psum | solution.py:174
  8.4 31.2 %copy-start.41 = (s32[4,256]{1,0:T(4,128)}, s32[4,256]{1,0:T(4,128)S(1)}, u32[]{:S(2)}) copy-start(s32[4,256]{1,0:T(4,128)S(1)} %eq.73) | copy-start | bytes 12292
  9.4 27.3 %copy-start.35 = (f32[1024]{0:T(1024)}, f32[1024]{0:T(1024)S(1)}, u32[]{:S(2)}) copy-start(f32[1024]{0:T(1024)S(1)} %get-tuple-element.596) | copy-start | bytes 12292
  15.8 5.3 copy-start.95
  20.3 3.6 copy-start.53
  33.4 110.2 %copy-start.3 = (f32[4,256,8,64]{1,3,2,0:T(8,128)}, f32[4,256,8,64]{1,3,2,0:T(8,128)S(1)}, u32[]{:S(2)}) copy-start(f32[4,256,8,64]{1,3,2,0:T(8,128)S(1)} %copy.116) | copy-start | bytes 6291460
  39.5 5.2 copy-start.11
  50.9 4.3 copy-start.88
  58.1 4.3 copy-start.88
  65.2 4.3 copy-start.88
  72.4 3.4 copy-start.94
  90.5 5.0 copy-start.92
  95.6 35.2 %copy-start.67 = (f32[512]{0:T(512)}, f32[512]{0:T(512)S(1)}, u32[]{:S(2)}) copy-start(f32[512]{0:T(512)S(1)} %mul.754) | copy-start | bytes 6148
  95.6 21.0 %copy-start.65 = (f32[512]{0:T(512)S(1)}, f32[512]{0:T(512)}, u32[]{:S(2)}) copy-start(f32[512]{0:T(512)} %param.36) | copy-start | bytes 6148
  115.9 93.4 %copy-start.37 = (f32[1024]{0:T(1024)}, f32[1024]{0:T(1024)S(1)}, u32[]{:S(2)}) copy-start(f32[1024]{0:T(1024)S(1)} %get-tuple-element.585) | copy-start | bytes 12292
  116.6 5.9 copy-start.99
  199.6 6.7 copy-start.16
  199.6 6.7 copy-start.79
  199.6 5.5 copy-start.12
  199.6 5.5 copy-start.21
  209.2 130.1 %reduce-scatter.2.cloned.1.call-start = ((), (), s32[]{:S(2)}) async-start(), calls=%async_computation.1 | async-start | bytes 5242880 | tf_op jit(solution)/shard_map/reduce_scatter | solution.py:148
  214.6 413.6 %all-gather.3.cloned.1.call-start = ((), (), s32[]{:S(2)}) async-start(), calls=%async_computation.3 | async-start | bytes 20971520 | tf_op jit(solution)/shard_map/all_gather | solution.py:180
  217.9 3.6 copy-start.15
  217.9 3.6 copy-start.30
  217.9 3.6 copy-start.33
  238.4 3.5 copy-start.40
  238.4 3.5 copy-start.54
  238.4 3.5 copy-start.55
  238.4 3.5 copy-start.56
  252.5 3.8 copy-start.9
  252.5 3.8 copy-start.36
  252.5 3.8 copy-start.68
  256.3 4.1 copy-start.60
  256.3 4.1 copy-start.62
  256.3 4.1 copy-start.64
  268.3 479.4 %all-reduce.34.cloned.1.call-start = ((), (), s32[]{:S(2)}) async-start(), calls=%async_computation.4 | async-start | bytes 14680064 | tf_op jit(solution)/shard_map/psum | solution.py:187
  270.3 3.9 copy-start.27
  279.6 4.2 copy-start.73
  279.6 4.2 copy-start.75
  279.6 4.2 copy-start.77
  628.2 10.3 %copy-start.46 = (f32[1024]{0:T(1024)S(1)}, f32[1024]{0:T(1024)}, u32[]{:S(2)}) copy-start(f32[1024]{0:T(1024)} %copy-done.45) | copy-start | bytes 12292
  628.2 10.3 %copy-start.52 = (f32[1024]{0:T(1024)S(1)}, f32[1024]{0:T(1024)}, u32[]{:S(2)}) copy-start(f32[1024]{0:T(1024)} %param.24) | copy-start | bytes 12292
  638.5 5.9 copy-start.87
  638.5 33.2 %copy-start.69 = (f32[1024]{0:T(1024)S(1)}, f32[1024]{0:T(1024)}, u32[]{:S(2)}) copy-start(f32[1024]{0:T(1024)} %get-tuple-element.582) | copy-start | bytes 12292
  (60 other events, 138.8 us)
Sparse Core Ops, SparseCore 0:
  209.3 51.5 all-reduce.31
  263.3 76.0 reduce-scatter.1
  340.9 287.2 all-gather.2
  632.8 114.9 all-reduce.33
